TPU v7x, 256 devices: a whole 4x4x8 slice. The times are simulated.
256 devices in a mesh: dp: 4 (over x), expert: 64 (over z, y, core).
Axes of the slice: x: 4, y: 4, z: 8, core: 2. Of those that a mesh axis runs over, the one named last changes fastest.
Arguments:
- hidden_acts: bfloat16 [4, 64, 1024, 768], P('dp', 'expert'), may hold values from -6 to 6
- out_grads: bfloat16 [4, 64, 1024, 2048], P('dp', 'expert'), may hold values from -0.29882812 to 0.29882812
- row_counts: int32 [4, 64], P('dp', 'expert'), may hold values from 128 to 1024, as said below
- plan_now: int32 [4, 64], replicated, may hold values from 0 to 23, as said below
- plan_next: int32 [4, 64], replicated, may hold values from 0 to 23, as said below
- master: float32 [24, 768, 2048], P(None, 'expert', 'dp'), may hold values from -6 to 6
- moment_one: float32 [24, 768, 2048], P(None, 'expert', 'dp'), may hold values from -6 to 6
- moment_two: float32 [24, 768, 2048], P(None, 'expert', 'dp'), may hold values from 0.01 to 0.3
Outputs:
- master_new: float32 [24, 768, 2048], P(None, 'expert', 'dp')
- moment_one_new: float32 [24, 768, 2048], P(None, 'expert', 'dp')
- moment_two_new: float32 [24, 768, 2048], P(None, 'expert', 'dp')
- replica_weights: bfloat16 [4, 64, 768, 2048], P('dp', 'expert')
Inputs may be any that keep to these rules, and one draw needn't show every extreme that they name: `plan_now`: every expert is named by 1 to 16 devices, and some expert by exactly 16. `plan_next`: every expert is named by 1 to 16 devices, and some expert by exactly 16. `row_counts`: A multiple of 128; rows from it on are padding. Some device has all 1024 rows live.
All inputs are finite; a program needn't handle non-finite values.
Results may differ from a plain program's by a relative error of at most 0.005.
Values may be sent and summed in bfloat16 or wider, within the bound.
A program may use at most 64 MiB of HBM per device.

v0:
```python
import jax
import jax.numpy as jnp
from jax import lax
from jax.sharding import PartitionSpec as P

beta_one = 0.9
beta_two = 0.999
learn_rate = 0.1
epsilon = 1e-08
first_fix = 1.0 - beta_one**10
second_fix = 1.0 - beta_two**10


def per_device(
    hidden_acts, out_grads, row_counts, plan_now, plan_next, master, moment_one, moment_two
):
    ex_count = lax.axis_size("expert")
    dp_index = lax.axis_index("dp")
    experts = master.shape[0]
    piece_rows = master.shape[1]
    hidden = hidden_acts[0, 0]
    upstream = out_grads[0, 0]
    width = upstream.shape[1]
    row_index = jnp.arange(hidden.shape[0], dtype=jnp.int32)
    row_mask = (row_index < row_counts[0, 0]).astype(hidden.dtype)[:, None]
    partial_value = lax.dot_general(
        hidden * row_mask, upstream, (((0,), (0,)), ((), ())), preferred_element_type=jnp.float32
    ).astype(jnp.bfloat16)
    expert_ids = jnp.arange(experts, dtype=jnp.int32)
    pieces = lax.all_to_all(
        partial_value.reshape(ex_count, piece_rows, width),
        "expert",
        split_axis=0,
        concat_axis=0,
        tiled=True,
    )
    sender_ids = lax.dynamic_index_in_dim(plan_now, dp_index, 0, keepdims=False)
    onehot = (sender_ids[None, :] == expert_ids[:, None]).astype(jnp.bfloat16)
    totals = jnp.einsum("es,srd->erd", onehot, pieces, preferred_element_type=jnp.float32)
    grad_sum = lax.psum_scatter(
        totals.astype(jnp.bfloat16), "dp", scatter_dimension=2, tiled=True
    ).astype(jnp.float32)
    moment_one_new = beta_one * moment_one + (1.0 - beta_one) * grad_sum
    moment_two_new = beta_two * moment_two + (1.0 - beta_two) * grad_sum * grad_sum
    master_new = master - learn_rate * (moment_one_new / first_fix) / (
        jnp.sqrt(moment_two_new / second_fix) + epsilon
    )
    rounded = master_new.astype(jnp.bfloat16)
    full_cols = lax.all_gather(rounded, "dp", axis=2, tiled=True)
    targets = lax.dynamic_index_in_dim(plan_next, dp_index, 0, keepdims=False)
    outgoing = jnp.take(full_cols, targets, axis=0)
    incoming = lax.all_to_all(outgoing, "expert", split_axis=0, concat_axis=0, tiled=True)
    replica = incoming.reshape(ex_count * piece_rows, width)
    return (master_new, moment_one_new, moment_two_new, replica[None, None])


def solution(mesh):
    return jax.shard_map(
        per_device,
        mesh=mesh,
        in_specs=(
            P("dp", "expert", None, None),
            P("dp", "expert", None, None),
            P("dp", "expert"),
            P(),
            P(),
            P(None, "expert", "dp"),
            P(None, "expert", "dp"),
            P(None, "expert", "dp"),
        ),
        out_specs=(
            P(None, "expert", "dp"),
            P(None, "expert", "dp"),
            P(None, "expert", "dp"),
            P("dp", "expert", None, None),
        ),
        check_vma=False,
    )
```

profile of v0, /device:TPU:8, one launch (start us, length us, event | category | flops | bytes accessed | tf_op | source)
XLA Modules:
  0.0 311.3 jit_solution(10174371553919339833)
XLA Ops:
  7.2 0.0 copy-start
  7.9 6.2 %fusion.2 = bf16[768,2048]{1,0:T(8,128)(2,1)S(1)} fusion(bf16[1,1,1024,2048]{3,2,1,0:T(8,128)(2,1)} %param.9, bf16[1,1,1024,768]{3,2,1,0:T(8,128)(2,1)} %param.8, bf16[1024]{0:T(1024)(128)(2,1)S(1)} %fusion.18), kind=kOutput, calls=%fused_computation.4 | convolution fusion | flops 3223584768 | bytes 8914944 | tf_op jit(solution)/shard_map/dot_general | solution.py:26
  14.1 2.7 reshape.58
  16.8 12.3 %all-to-all-start = ((bf16[64,12,2048]{2,1,0:T(8,128)(2,1)}), bf16[64,12,2048]{2,1,0:T(8,128)(2,1)}, u32[]{:S(2)}, u32[]{:S(2)}) async-start(bf16[64,12,2048]{2,1,0:T(8,128)(2,1)} %reshape.58), calls=%async_computation | async-start | bytes 8388608 | tf_op jit(solution)/shard_map/all_to_all | solution.py:30
  29.1 0.0 copy-start.1
  29.1 0.0 copy-start.2
  29.1 0.0 copy-start.3
  29.1 0.0 reduce-scatter.2.cloned.1.call-start
  29.2 0.0 copy-done
  29.2 0.0 copy-start.4
  29.2 96.0 %all-to-all-done = bf16[64,12,2048]{2,1,0:T(8,128)(2,1)} async-done(((bf16[64,12,2048]{2,1,0:T(8,128)(2,1)}), bf16[64,12,2048]{2,1,0:T(8,128)(2,1)}, u32[]{:S(2)}, u32[]{:S(2)}) %all-to-all-start) | async-done | bytes 3145760 | tf_op jit(solution)/shard_map/all_to_all | solution.py:30
  125.2 6.6 %fusion.7 = bf16[24,12,2048]{2,0,1:T(8,128)(2,1)} fusion(bf16[64,12,2048]{2,1,0:T(8,128)(2,1)} %all-to-all-done, s32[64]{0:T(128)S(1)} %dynamic-slice_bitcast_fusion), kind=kOutput, calls=%fused_computation.7 | convolution fusion | flops 76088832 | bytes 4325632 | tf_op jit(solution)/shard_map/es,srd->erd/dot_general | solution.py:39
  131.9 0.0 reduce-scatter.2.cloned.1.call-update
  131.9 0.0 all-gather.2.cloned.1.call-start
  131.9 22.9 %reduce-scatter.2.cloned.1.call-done = bf16[24,12,512]{2,0,1:T(8,128)(2,1)} async-done(((bf16[24,12,2048]{2,0,1:T(8,128)(2,1)}), bf16[24,12,512]{2,0,1:T(8,128)(2,1)}) %reduce-scatter.2.cloned.1.call-update) | async-done | bytes 294928 | tf_op jit(solution)/shard_map/reduce_scatter | solution.py:40
  154.8 0.0 copy-done.1
  154.8 0.0 copy-done.2
  154.8 0.0 copy-done.3
  154.8 2.5 fusion.20
  157.4 0.0 all-gather.2.cloned.1.call-update
  157.4 0.0 copy-done.4
  157.5 26.8 %all-gather.2.cloned.1.call-done = bf16[24,12,2048]{2,0,1:T(8,128)(2,1)} async-done(((bf16[24,12,512]{2,0,1:T(8,128)(2,1)}), bf16[24,12,2048]{2,0,1:T(8,128)(2,1)}) %all-gather.2.cloned.1.call-update) | async-done | bytes 1179664 | tf_op jit(solution)/shard_map/all_gather | solution.py:49
  184.3 1.9 copy.16
  186.2 2.8 gather_fusion
  189.0 2.6 broadcast_select_fusion
  191.6 106.7 %all_to_all.10 = bf16[64,12,2048]{2,1,0:T(8,128)(2,1)} all-to-all(bf16[64,12,2048]{2,1,0:T(8,128)(2,1)S(1)} %broadcast_select_fusion), channel_id=1, replica_groups=mesh['dp'=4,'expert'=64] {'expert'}, dimensions={0} | all-to-all | bytes 6291456 | tf_op jit(solution)/shard_map/all_to_all | solution.py:52
  298.3 6.2 %broadcast_in_dim_reshape.3 = bf16[1,1,768,2048]{3,2,1,0:T(8,128)(2,1)} reshape(bf16[64,12,2048]{2,1,0:T(8,128)(2,1)} %all_to_all.10) | data formatting | bytes 6291456 | tf_op jit(solution)/shard_map/broadcast_in_dim;reshape | solution.py:54
  (5 shorter events, 0.0 us)
Async XLA Ops:
  7.2 22.0 %copy-start = (s32[4,64]{1,0:T(4,128)S(1)}, s32[4,64]{1,0:T(4,128)}, u32[]{:S(2)}) copy-start(s32[4,64]{1,0:T(4,128)} %param.11) | copy-start | bytes 3076
  16.8 108.4 %all-to-all-start = ((bf16[64,12,2048]{2,1,0:T(8,128)(2,1)}), bf16[64,12,2048]{2,1,0:T(8,128)(2,1)}, u32[]{:S(2)}, u32[]{:S(2)}) async-start(bf16[64,12,2048]{2,1,0:T(8,128)(2,1)} %reshape.58), calls=%async_computation | async-start | bytes 8388608 | tf_op jit(solution)/shard_map/all_to_all | solution.py:30
  29.1 125.7 %copy-start.1 = (f32[24,12,512]{2,0,1:T(8,128)S(1)}, f32[24,12,512]{2,0,1:T(8,128)}, u32[]{:S(2)}) copy-start(f32[24,12,512]{2,0,1:T(8,128)} %param.13) | copy-start | bytes 1769476
  29.1 125.7 %copy-start.2 = (f32[24,12,512]{2,0,1:T(8,128)S(1)}, f32[24,12,512]{2,0,1:T(8,128)}, u32[]{:S(2)}) copy-start(f32[24,12,512]{2,0,1:T(8,128)} %param.14) | copy-start | bytes 1769476
  29.1 125.7 %copy-start.3 = (f32[24,12,512]{2,0,1:T(8,128)S(1)}, f32[24,12,512]{2,0,1:T(8,128)}, u32[]{:S(2)}) copy-start(f32[24,12,512]{2,0,1:T(8,128)} %param.15) | copy-start | bytes 1769476
  29.1 125.7 %reduce-scatter.2.cloned.1.call-start = ((), (), s32[]{:S(2)}) async-start(), calls=%async_computation.3 | async-start | bytes 1474560 | tf_op jit(solution)/shard_map/reduce_scatter | solution.py:40
  29.2 128.2 %copy-start.4 = (s32[4,64]{1,0:T(4,128)S(1)}, s32[4,64]{1,0:T(4,128)}, u32[]{:S(2)}) copy-start(s32[4,64]{1,0:T(4,128)} %param.12) | copy-start | bytes 3076
  131.9 52.4 %all-gather.2.cloned.1.call-start = ((), (), s32[]{:S(2)}) async-start(), calls=%async_computation.4 | async-start | bytes 1474560 | tf_op jit(solution)/shard_map/all_gather | solution.py:49
Sparse Core Ops, SparseCore 0:
  132.0 22.7 reduce-scatter.1
  157.5 26.6 all-gather.1
where the time goes:
time: 312 us; the launch traced here: 311 us
  waiting for transfers between devices  146 us (47%)
  blocking collectives  107 us (34%)
  between operations  14.8 us (5%)
  local copies, waits for them, and re-layouts  13.6 us (4%)
  matrix products  12.9 us (4%)
  starting transfers between devices  12.4 us (4%)
  other arithmetic  5.2 us (2%)
    all_to_all x1, blocking collectives, per_device(): lax.all_to_all(outgoing, 'expert', split_axis=0, concat_axis=0, tiled=True)  107 us
    all_to_all x1, waiting for transfers between devices, per_device(): lax.all_to_all(partial_value.reshape(ex_count, piece_rows, width), 'exper...  96 us
    all_gather x1, waiting for transfers between devices, per_device(): full_cols = lax.all_gather(rounded, 'dp', axis=2, tiled=True)  26.8 us
    reduce_scatter x1, waiting for transfers between devices, per_device(): lax.psum_scatter(totals.astype(jnp.bfloat16), 'dp', scatter_dimension=2,...  22.9 us
    all_to_all x1, starting transfers between devices, per_device(): lax.all_to_all(partial_value.reshape(ex_count, piece_rows, width), 'exper...  12.3 us
    dot_general x1, matrix products, per_device(): jnp.einsum('es,srd->erd', onehot, pieces, preferred_element_type=jnp.floa...  6.64 us
  transfers between devices with their start and end apart: 3, of which 3 were waited for; matrix products, arithmetic and copies ran while one was open for 0% of the time, Pallas kernels for 0%

commit v1 on v0

--- a/solution.py
+++ b/solution.py
@@ -46,7 +46,25 @@
         jnp.sqrt(moment_two_new / second_fix) + epsilon
     )
     rounded = master_new.astype(jnp.bfloat16)
-    full_cols = lax.all_gather(rounded, "dp", axis=2, tiled=True)
+    size, index, extent = (lax.axis_size("dp"), lax.axis_index("dp"), rounded.shape[2])
+    ahead = [(i, (i + 1) % size) for i in range(size)]
+    left = [(i, (i - 1) % size) for i in range(size)]
+    full_cols = jnp.zeros(
+        (*rounded.shape[:2], size * extent, *rounded.shape[2 + 1 :]), rounded.dtype
+    )
+    full_cols = lax.dynamic_update_slice_in_dim(full_cols, rounded, index * extent, axis=2)
+    from_left = from_right = rounded
+    halfway = size // 2
+    for step in range(1, halfway + 1):
+        from_left = lax.ppermute(from_left, "dp", ahead)
+        full_cols = lax.dynamic_update_slice_in_dim(
+            full_cols, from_left, (index - step) % size * extent, axis=2
+        )
+        if step < size - halfway:
+            from_right = lax.ppermute(from_right, "dp", left)
+            full_cols = lax.dynamic_update_slice_in_dim(
+                full_cols, from_right, (index + step) % size * extent, axis=2
+            )
     targets = lax.dynamic_index_in_dim(plan_next, dp_index, 0, keepdims=False)
     outgoing = jnp.take(full_cols, targets, axis=0)
     incoming = lax.all_to_all(outgoing, "expert", split_axis=0, concat_axis=0, tiled=True)

time: 312 us -> 300 us (0.962)
  waiting for transfers between devices: 146 us -> 132 us
  starting transfers between devices: 12.4 us -> 15.6 us
    all_gather x1 -> x0, waiting for transfers between devices: 26.8 us -> none  [per_device(): full_cols = lax.all_gather(rounded, 'dp', axis=2, tiled=True)]
    ppermute x0 -> x3, waiting for transfers between devices: none -> 12.8 us  [the longest x2 12.8 us: per_device(): from_left = lax.ppermute(from_left, 'dp', ahead)]
    ppermute x0 -> x3, starting transfers between devices: none -> 3.32 us  [the longest x1 3.31 us: per_device(): from_right = lax.ppermute(from_right, 'dp', left)]
  transfers between devices with their start and end apart: 3 -> 5, of which waited for: 3 -> 4; matrix products, arithmetic and copies ran while one was open for 0% -> 0% of each run, Pallas kernels for 0% -> 0%
where the time goes in v1:
time: 300 us; the launch traced here: 299 us
  waiting for transfers between devices  132 us (44%)
  blocking collectives  107 us (36%)
  starting transfers between devices  15.6 us (5%)
  between operations  14.9 us (5%)
  matrix products  12.9 us (4%)
  local copies, waits for them, and re-layouts  12.3 us (4%)
  other arithmetic  5.1 us (2%)
    all_to_all x1, blocking collectives, per_device(): lax.all_to_all(outgoing, 'expert', split_axis=0, concat_axis=0, tiled=True)  107 us
    all_to_all x1, waiting for transfers between devices, per_device(): lax.all_to_all(partial_value.reshape(ex_count, piece_rows, width), 'exper...  96 us
    reduce_scatter x1, waiting for transfers between devices, per_device(): lax.psum_scatter(totals.astype(jnp.bfloat16), 'dp', scatter_dimension=2,...  22.9 us
    ppermute x2, waiting for transfers between devices, per_device(): from_left = lax.ppermute(from_left, 'dp', ahead)  12.8 us
    all_to_all x1, starting transfers between devices, per_device(): lax.all_to_all(partial_value.reshape(ex_count, piece_rows, width), 'exper...  12.3 us
    dot_general x1, matrix products, per_device(): jnp.einsum('es,srd->erd', onehot, pieces, preferred_element_type=jnp.floa...  6.64 us
    dot_general x1, matrix products, per_device(): lax.dot_general(hidden * row_mask, upstream, (((0,), (0,)), ((), ())), pr...  6.23 us
    another operation x1, local copies, waits for them, and re-layouts, per_device(): return (master_new, moment_one_new, moment_two_new, replica[None, None])  6.15 us
  transfers between devices with their start and end apart: 5, of which 4 were waited for; matrix products, arithmetic and copies ran while one was open for 0% of the time, Pallas kernels for 0%

profile of v1, /device:TPU:8, one launch (start us, length us, event | category | flops | bytes accessed | tf_op | source)
XLA Modules:
  0.0 299.2 jit_solution(3391603351303924301)
XLA Ops:
  7.2 0.0 copy-start
  7.9 6.2 %fusion.2 = bf16[768,2048]{1,0:T(8,128)(2,1)S(1)} fusion(bf16[1,1,1024,2048]{3,2,1,0:T(8,128)(2,1)} %param.9, bf16[1,1,1024,768]{3,2,1,0:T(8,128)(2,1)} %param.8, bf16[1024]{0:T(1024)(128)(2,1)S(1)} %fusion.18), kind=kOutput, calls=%fused_computation.4 | convolution fusion | flops 3223584768 | bytes 8914944 | tf_op jit(solution)/shard_map/dot_general | solution.py:26
  14.1 2.7 reshape.58
  16.8 12.3 %all-to-all-start = ((bf16[64,12,2048]{2,1,0:T(8,128)(2,1)}), bf16[64,12,2048]{2,1,0:T(8,128)(2,1)}, u32[]{:S(2)}, u32[]{:S(2)}) async-start(bf16[64,12,2048]{2,1,0:T(8,128)(2,1)} %reshape.58), calls=%async_computation | async-start | bytes 8388608 | tf_op jit(solution)/shard_map/all_to_all | solution.py:30
  29.1 0.0 reduce-scatter.2.cloned.1.call-start
  29.2 0.0 copy-done
  29.2 0.0 copy-start.4
  29.2 0.0 copy-start.1
  29.2 0.0 copy-start.2
  29.2 0.0 copy-start.3
  29.2 96.0 %all-to-all-done = bf16[64,12,2048]{2,1,0:T(8,128)(2,1)} async-done(((bf16[64,12,2048]{2,1,0:T(8,128)(2,1)}), bf16[64,12,2048]{2,1,0:T(8,128)(2,1)}, u32[]{:S(2)}, u32[]{:S(2)}) %all-to-all-start) | async-done | bytes 3145760 | tf_op jit(solution)/shard_map/all_to_all | solution.py:30
  125.2 6.6 %fusion.7 = bf16[24,12,2048]{2,0,1:T(8,128)(2,1)} fusion(bf16[64,12,2048]{2,1,0:T(8,128)(2,1)} %all-to-all-done, s32[64]{0:T(128)S(1)} %fusion.19), kind=kOutput, calls=%fused_computation.7 | convolution fusion | flops 76088832 | bytes 4325632 | tf_op jit(solution)/shard_map/es,srd->erd/dot_general | solution.py:39
  131.9 0.0 reduce-scatter.2.cloned.1.call-update
  131.9 0.0 copy-done.4
  131.9 22.9 %reduce-scatter.2.cloned.1.call-done = bf16[24,12,512]{2,0,1:T(8,128)(2,1)} async-done(((bf16[24,12,2048]{2,0,1:T(8,128)(2,1)}), bf16[24,12,512]{2,0,1:T(8,128)(2,1)}) %reduce-scatter.2.cloned.1.call-update) | async-done | bytes 294928 | tf_op jit(solution)/shard_map/reduce_scatter | solution.py:40
  154.8 0.0 copy-done.1
  154.8 0.0 copy-done.2
  154.8 0.0 copy-done.3
  154.8 2.4 fusion.21
  157.3 0.0 collective-permute-start
  157.4 3.3 %collective-permute-start.1 = (bf16[24,12,512]{2,0,1:T(8,128)(2,1)S(1)}, bf16[24,12,512]{2,0,1:T(8,128)(2,1)S(1)}, u32[]{:S(2)}, u32[]{:S(2)}) collective-permute-start(bf16[24,12,512]{2,0,1:T(8,128)(2,1)S(1)} %get-tuple-element.4), channel_id=1, source_target_pairs={{0,192},{64,0},{128,64},{192,128},{1,193},{65,1},{129,65},{193,129... | collective-permute-start | bytes 884744 | tf_op jit(solution)/shard_map/ppermute | solution.py:64
  160.7 0.2 broadcast_in_dim.17
  160.9 0.1 copy_dynamic-update-slice_fusion.3
  161.0 5.1 %collective-permute-done = bf16[24,12,512]{2,0,1:T(8,128)(2,1)S(1)} collective-permute-done((bf16[24,12,512]{2,0,1:T(8,128)(2,1)S(1)}, bf16[24,12,512]{2,0,1:T(8,128)(2,1)S(1)}, u32[]{:S(2)}, u32[]{:S(2)}) %collective-permute-start) | collective-permute-done | bytes 294944 | tf_op jit(solution)/shard_map/ppermute | solution.py:59
  166.1 0.0 collective-permute-start.2
  166.1 0.1 copy_dynamic-update-slice_fusion.2
  166.2 0.0 collective-permute-done.1
  166.2 0.1 copy_dynamic-update-slice_fusion.1
  166.3 7.7 %collective-permute-done.2 = bf16[24,12,512]{2,0,1:T(8,128)(2,1)S(1)} collective-permute-done((bf16[24,12,512]{2,0,1:T(8,128)(2,1)S(1)}, bf16[24,12,512]{2,0,1:T(8,128)(2,1)S(1)}, u32[]{:S(2)}, u32[]{:S(2)}) %collective-permute-start.2) | collective-permute-done | bytes 294944 | tf_op jit(solution)/shard_map/ppermute | solution.py:59
  174.0 0.1 copy_dynamic-update-slice_fusion
  174.1 2.8 gather_fusion
  176.9 2.6 broadcast_select_fusion
  179.5 106.7 %all_to_all.10 = bf16[64,12,2048]{2,1,0:T(8,128)(2,1)} all-to-all(bf16[64,12,2048]{2,1,0:T(8,128)(2,1)S(1)} %broadcast_select_fusion), channel_id=1, replica_groups=mesh['dp'=4,'expert'=64] {'expert'}, dimensions={0} | all-to-all | bytes 6291456 | tf_op jit(solution)/shard_map/all_to_all | solution.py:70
  286.2 6.2 %broadcast_in_dim_reshape.3 = bf16[1,1,768,2048]{3,2,1,0:T(8,128)(2,1)} reshape(bf16[64,12,2048]{2,1,0:T(8,128)(2,1)} %all_to_all.10) | data formatting | bytes 6291456 | tf_op jit(solution)/shard_map/broadcast_in_dim;reshape | solution.py:72
  (5 shorter events, 0.0 us)
Async XLA Ops:
  7.2 22.0 %copy-start = (s32[4,64]{1,0:T(4,128)S(1)}, s32[4,64]{1,0:T(4,128)}, u32[]{:S(2)}) copy-start(s32[4,64]{1,0:T(4,128)} %param.11) | copy-start | bytes 3076
  16.8 108.4 %all-to-all-start = ((bf16[64,12,2048]{2,1,0:T(8,128)(2,1)}), bf16[64,12,2048]{2,1,0:T(8,128)(2,1)}, u32[]{:S(2)}, u32[]{:S(2)}) async-start(bf16[64,12,2048]{2,1,0:T(8,128)(2,1)} %reshape.58), calls=%async_computation | async-start | bytes 8388608 | tf_op jit(solution)/shard_map/all_to_all | solution.py:30
  29.1 125.7 %reduce-scatter.2.cloned.1.call-start = ((), (), s32[]{:S(2)}) async-start(), calls=%async_computation.3 | async-start | bytes 1474560 | tf_op jit(solution)/shard_map/reduce_scatter | solution.py:40
  29.2 102.7 %copy-start.4 = (s32[4,64]{1,0:T(4,128)S(1)}, s32[4,64]{1,0:T(4,128)}, u32[]{:S(2)}) copy-start(s32[4,64]{1,0:T(4,128)} %param.12) | copy-start | bytes 3076
  29.2 125.6 %copy-start.1 = (f32[24,12,512]{2,0,1:T(8,128)S(1)}, f32[24,12,512]{2,0,1:T(8,128)}, u32[]{:S(2)}) copy-start(f32[24,12,512]{2,0,1:T(8,128)} %param.13) | copy-start | bytes 1769476
  29.2 125.6 %copy-start.2 = (f32[24,12,512]{2,0,1:T(8,128)S(1)}, f32[24,12,512]{2,0,1:T(8,128)}, u32[]{:S(2)}) copy-start(f32[24,12,512]{2,0,1:T(8,128)} %param.14) | copy-start | bytes 1769476
  29.2 125.6 %copy-start.3 = (f32[24,12,512]{2,0,1:T(8,128)S(1)}, f32[24,12,512]{2,0,1:T(8,128)}, u32[]{:S(2)}) copy-start(f32[24,12,512]{2,0,1:T(8,128)} %param.15) | copy-start | bytes 1769476
  157.3 8.8 %collective-permute-start = (bf16[24,12,512]{2,0,1:T(8,128)(2,1)S(1)}, bf16[24,12,512]{2,0,1:T(8,128)(2,1)S(1)}, u32[]{:S(2)}, u32[]{:S(2)}) collective-permute-start(bf16[24,12,512]{2,0,1:T(8,128)(2,1)S(1)} %get-tuple-element.4), channel_id=1, source_target_pairs={{0,64},{64,128},{128,192},{192,0},{1,65},{65,129},{129,193},{193,1... | collective-permute-start | bytes 884744 | tf_op jit(solution)/shard_map/ppermute | solution.py:59
  157.4 8.8 %collective-permute-start.1 = (bf16[24,12,512]{2,0,1:T(8,128)(2,1)S(1)}, bf16[24,12,512]{2,0,1:T(8,128)(2,1)S(1)}, u32[]{:S(2)}, u32[]{:S(2)}) collective-permute-start(bf16[24,12,512]{2,0,1:T(8,128)(2,1)S(1)} %get-tuple-element.4), channel_id=1, source_target_pairs={{0,192},{64,0},{128,64},{192,128},{1,193},{65,1},{129,65},{193,129... | collective-permute-start | bytes 884744 | tf_op jit(solution)/shard_map/ppermute | solution.py:64
  166.1 7.9 %collective-permute-start.2 = (bf16[24,12,512]{2,0,1:T(8,128)(2,1)S(1)}, bf16[24,12,512]{2,0,1:T(8,128)(2,1)S(1)}, u32[]{:S(2)}, u32[]{:S(2)}) collective-permute-start(bf16[24,12,512]{2,0,1:T(8,128)(2,1)S(1)} %collective-permute-done), channel_id=1, source_target_pairs={{0,64},{64,128},{128,192},{192,0},{1,65},{65,129},{129,193},{193,1... | collective-permute-start | bytes 884744 | tf_op jit(solution)/shard_map/ppermute | solution.py:59
Sparse Core Ops, SparseCore 0:
  132.0 22.7 reduce-scatter.1
